TPU v7x, 32 devices: a whole 2x2x4 slice. The times are simulated.
32 devices in a mesh: seq: 4 (over y, x), dp: 4 (over z), enc: 2 (over core).
Axes of the slice: x: 2, y: 2, z: 4, core: 2. Of those that a mesh axis runs over, the one named last changes fastest.
Arguments:
- lm_grad: bfloat16 [4, 4, 192, 1152], P('dp', 'enc', 'seq'), may hold values from -6 to 6
- image_tokens: int32 [4, 4, 4], P('dp'), may hold values from 1 to 15, as said below
- image_offset: int32 [4, 4, 4], P('dp'), may hold values from 0 to 47, as said below
- image_owner: int32 [4, 4, 4], P('dp'), may hold values from 0 to 3, as said below
- mlp_input: bfloat16 [4, 4, 240, 1152], P('dp', None, 'seq'), may hold values from -36 to 36
- layer_output: bfloat16 [4, 4, 240, 1152], P('dp', 'enc', 'seq'), may hold values from -36 to 36
- pre_gain: float32 [1152], replicated, may hold values from 0.5 to 1.5
- pre_bias: float32 [1152], replicated, may hold values from -3 to 3
- fc1_weight: bfloat16 [1152, 4304], P(None, 'enc'), may hold values from -0.1875 to 0.1875
- fc1_bias: float32 [4304], P('enc'), may hold values from -3 to 3
- fc2_weight: bfloat16 [4304, 1152], P('enc'), may hold values from -0.09375 to 0.09375
- post_gain: float32 [1152], replicated, may hold values from 0.5 to 1.5
- post_bias: float32 [1152], replicated, may hold values from -3 to 3
- merge_gain: float32 [1152], replicated, may hold values from 0.5 to 1.5
Outputs:
- act_grad: bfloat16 [4, 4, 240, 1152], P('dp', 'enc', 'seq')
- norm_grads: float32 [6, 1152], replicated
- fc1_bias_grad: float32 [4304], replicated
Inputs may be any that keep to these rules, and one draw needn't show every extreme that they name: `image_tokens`: the 4 images of one LM shard have token counts that sum to 48, and one of them has 15. `image_offset`: the images of one LM shard lie back to back over its 48 rows, in some order; each entry is an image's first row in its shard. Images are placed round-robin by their index j in a shard: image_owner[r, q, j] = (q + image_owner[r, 0, j]) mod 4, with the 4 values image_owner[r, 0, j] different. So each encoder chip owns exactly 4 images of its replica, the visual tokens owned by one chip number at most 60, and some chip owns exactly 60.
All inputs are finite; a program needn't handle non-finite values.
Results may differ from a plain program's by a relative error of at most 0.005.
Values may be sent and summed in bfloat16 or wider, within the bound.
A program may use at most 64 MiB of HBM per device.

v0:
```python
import math
import jax
import jax.numpy as jnp
from jax import lax
from jax.sharding import PartitionSpec as P

D = 1152
FF = 4304
PATCH_GROUP = 4
ROWS_DEV = 48
CAP_TOK = 60
EPSILON = 1e-06
SLOPE_K = math.sqrt(2.0 / math.pi)
CUBIC = 0.044715


def layer_norm(values):
    row_mean = jnp.mean(values, axis=-1, keepdims=True)
    centred = values - row_mean
    return centred * lax.rsqrt(jnp.mean(centred * centred, axis=-1, keepdims=True) + EPSILON)


def rms_norm(values):
    return values * lax.rsqrt(jnp.mean(values * values, axis=-1, keepdims=True) + EPSILON)


def gelu_slope(pre_act):
    inner_arg = SLOPE_K * (pre_act + CUBIC * pre_act * pre_act * pre_act)
    tangent = jnp.tanh(inner_arg)
    return 0.5 * (1.0 + tangent) + 0.5 * pre_act * (1.0 - tangent * tangent) * SLOPE_K * (
        1.0 + 3.0 * CUBIC * pre_act * pre_act
    )


def head_back(incoming, layer_rows, merge_gain, post_gain, post_bias):

    def merge_head(row_values, merge_scale, post_scale, post_shift):
        return rms_norm(layer_norm(row_values) * post_scale + post_shift) * merge_scale

    _, pullback = jax.vjp(
        merge_head, layer_rows.astype(jnp.float32), merge_gain, post_gain, post_bias
    )
    return pullback(incoming.astype(jnp.float32))


def pre_back(input_rows, pre_gain, pre_bias, upstream):

    def prenorm(row_values, scale_vec, shift_vec):
        return layer_norm(row_values) * scale_vec + shift_vec

    _, pullback = jax.vjp(prenorm, input_rows.astype(jnp.float32), pre_gain, pre_bias)
    return pullback(upstream)


def slot_source(lengths, offsets, owners, chip_index):
    shard_count = lengths.shape[0]
    is_mine = owners == chip_index
    my_len = jnp.sum(jnp.where(is_mine, lengths, 0), axis=1)
    my_off = jnp.sum(jnp.where(is_mine, offsets, 0), axis=1)
    slot_first = jnp.cumsum(my_len) - my_len
    slot_ids = jnp.arange(CAP_TOK, dtype=jnp.int32)
    inside = (slot_ids[:, None] >= slot_first[None, :]) & (
        slot_ids[:, None] < (slot_first + my_len)[None, :]
    )
    live_slot = jnp.any(inside, axis=1)
    shard_ids = jnp.arange(shard_count, dtype=jnp.int32)
    source = jnp.sum(jnp.where(inside, shard_ids[None, :], 0), axis=1)
    token_index = slot_ids - jnp.sum(jnp.where(inside, slot_first[None, :], 0), axis=1)
    shard_row = jnp.sum(jnp.where(inside, my_off[None, :], 0), axis=1) + token_index
    return (live_slot, source, token_index, shard_row)


def body(
    lm_grad,
    image_tokens,
    image_offset,
    image_owner,
    mlp_input,
    layer_output,
    pre_gain,
    pre_bias,
    fc1_weight,
    fc1_bias,
    fc2_weight,
    post_gain,
    post_bias,
    merge_gain,
):
    chip_index = lax.axis_index("seq")
    core_index = lax.axis_index("enc")
    shards = lax.axis_size("seq")
    own_patches = PATCH_GROUP // lax.axis_size("enc")
    lengths = image_tokens[0]
    offsets = image_offset[0]
    owners = image_owner[0]
    live_slot, source, token_index, shard_row = slot_source(lengths, offsets, owners, chip_index)
    own_rows = lm_grad[0]
    global_row = source * ROWS_DEV + shard_row
    portion = lax.all_gather(own_rows, "seq", axis=1, tiled=True)
    row_count = portion.shape[1]
    inside_piece = live_slot & (global_row >= 0) & (global_row < row_count)
    taken = jnp.take(portion, jnp.clip(global_row, 0, row_count - 1), axis=1)
    incoming = jnp.where(inside_piece[None, :, None], taken, jnp.zeros_like(taken))
    res_grad, merge_grad, post_grad, shift_grad = head_back(
        incoming, layer_output[0], merge_gain, post_gain, post_bias
    )
    res_wire = res_grad.astype(jnp.bfloat16)
    all_res = lax.all_gather(res_wire, "enc", axis=0, tiled=True)
    input_rows = mlp_input[0]
    normed = (layer_norm(input_rows.astype(jnp.float32)) * pre_gain + pre_bias).astype(jnp.bfloat16)
    pre_act = (
        jnp.dot(normed.reshape(-1, D), fc1_weight, preferred_element_type=jnp.float32) + fc1_bias
    )
    down_back = lax.dot_general(
        all_res.reshape(-1, D),
        fc2_weight,
        (((1,), (1,)), ((), ())),
        preferred_element_type=jnp.float32,
    )
    hidden_grad = down_back * gelu_slope(pre_act)
    fc1_part = jnp.sum(hidden_grad, axis=0)
    hidden_units = fc1_bias.shape[0]
    hidden_wire = hidden_grad.astype(jnp.bfloat16).reshape(PATCH_GROUP, CAP_TOK, hidden_units)
    portion = hidden_wire
    product = lax.dot_general(
        portion.reshape(-1, hidden_units),
        fc1_weight,
        (((1,), (1,)), ((), ())),
        preferred_element_type=jnp.float32,
    )
    summed = lax.psum(product.reshape(PATCH_GROUP, CAP_TOK, D), "enc")
    upstream = lax.dynamic_slice_in_dim(summed, core_index * own_patches, own_patches, 0)
    own_input = lax.dynamic_slice_in_dim(input_rows, core_index * own_patches, own_patches, 0)
    input_grad, pre_scale_grad, pre_shift_grad = pre_back(own_input, pre_gain, pre_bias, upstream)
    act_grad = (res_grad + input_grad).astype(jnp.bfloat16)[None]
    fc2_part = jnp.sum(res_grad, axis=(0, 1))
    norm_part = jnp.stack(
        [merge_grad, post_grad, shift_grad, fc2_part, pre_scale_grad, pre_shift_grad]
    )
    fc1_full = lax.dynamic_update_slice_in_dim(
        jnp.zeros((FF,), jnp.float32), fc1_part, core_index * hidden_units, 0
    )
    norm_sum, fc1_sum = lax.psum((norm_part, fc1_full), ("seq", "dp", "enc"))
    grad_scale = 1.0 / math.sqrt(PATCH_GROUP * ROWS_DEV * shards * lax.axis_size("dp"))
    return (act_grad, norm_sum * grad_scale, fc1_sum * grad_scale)


def solution(mesh):
    in_specs = (
        P("dp", "enc", "seq", None),
        P("dp", None, None),
        P("dp", None, None),
        P("dp", None, None),
        P("dp", None, "seq", None),
        P("dp", "enc", "seq", None),
        P(),
        P(),
        P(None, "enc"),
        P("enc"),
        P("enc", None),
        P(),
        P(),
        P(),
    )
    out_specs = (P("dp", "enc", "seq", None), P(), P())
    return jax.shard_map(body, mesh=mesh, in_specs=in_specs, out_specs=out_specs, check_vma=False)
```

profile of v0, /device:TPU:0, one launch (start us, length us, event | category | flops | bytes accessed | tf_op | source)
XLA Modules:
  0.0 126.4 jit_solution(4036860565229651967)
XLA Ops:
  7.2 0.9 select_reduce_fusion.2
  8.5 1.3 %convert_reduce_fusion.2 = f32[4,60]{0,1:T(8,128)S(1)} fusion(bf16[1,4,60,1152]{3,1,2,0:T(4,128)(2,1)} %param.18), kind=kLoop, calls=%fused_computation.44 | loop fusion | flops 552720 | bytes 553920 | tf_op jit(solution)/shard_map/reduce_sum | solution.py:18
  9.9 1.6 %fusion.6 = f32[4,60]{0,1:T(8,128)S(1)} fusion(bf16[1,4,60,1152]{3,1,2,0:T(4,128)(2,1)} %param.18, f32[4,60]{0,1:T(8,128)S(1)} %broadcast_multiply_fusion.2), kind=kLoop, calls=%fused_computation.12 | loop fusion | flops 1105680 | bytes 554880 | tf_op jit(solution)/shard_map/reduce_sum | solution.py:20
  11.6 1.1 copy.66
  12.9 13.7 %all-gather = bf16[1,2,192,1152]{3,1,0,2:T(2,128)(2,1)S(1)} all-gather(bf16[1,2,48,1152]{3,1,0,2:T(2,128)(2,1)S(1)} %copy.52), channel_id=2, replica_groups=mesh['seq'=4,'dp'=4,'enc'=2] {'seq'}, dimensions={2}, use_global_device_ids=true | all-gather | bytes 1105920 | tf_op jit(solution)/shard_map/all_gather | solution.py:99
  26.9 0.5 fusion.14
  27.6 0.7 multiply_reduce_fusion.1
  28.6 1.2 gather_fusion
  29.7 1.7 %fusion.27 = (f32[1152]{0:T(1024)S(1)}, f32[2,60]{0,1:T(8,128)S(1)}, bf16[60,2,1152]{2,1,0:T(2,128)(2,1)S(1)}) fusion(f32[2,60]{0,1:T(8,128)S(1)} %copy.58, f32[1152]{0:T(1024)S(1)} %copy-done.4, f32[1152]{0:T(1024)S(1)} %copy-done.3, f32[2,60]{0,1:T(8,128)S(1)} %copy.56, f32[2,60]{0,1:T(8,128)S(1)} %broadcast_multiply_fusion.3, ...), kind=kLoop, calls=%fused_computation.43 | loop fusion | flops 1934088 | bytes 849912 | tf_op jit(solution)/shard_map/transpose(jvp())/reduce_sum | solution.py:38
  31.7 1.9 %multiply_reduce_fusion = (f32[1152]{0:T(1024)S(1)}, f32[2,60]{0,1:T(8,128)S(1)}, f32[1152]{0:T(1024)S(1)}, f32[2,60,1152]{2,0,1:T(2,128)S(1)}) fusion(bf16[1,2,60,1152]{3,1,2,0:T(2,128)(2,1)S(1)} %copy-done.1, f32[2,60]{0,1:T(8,128)S(1)} %copy.56, f32[2,60]{0,1:T(8,128)S(1)} %broadcast_multiply_fusion.3, f32[1152]{0:T(1024)S(1)} %copy-done.3, ...), kind=kLoop, calls=%fused_computation.45 | loop fusion | flops 2347656 | bytes 1131360 | tf_op jit(solution)/shard_map/transpose(jvp())/reduce_sum | solution.py:38
  33.8 0.8 fusion.42
  35.1 2.5 %all_gather.7 = bf16[4,60,1152]{2,1,0:T(8,128)(2,1)S(1)} all-gather(bf16[2,60,1152]{2,1,0:T(8,128)(2,1)S(1)} %copy.65), channel_id=1, replica_groups=mesh['seq'=4,'dp'=4,'enc'=2] {'enc'}, dimensions={0}, use_global_device_ids=true | all-gather | bytes 829440 | tf_op jit(solution)/shard_map/all_gather | solution.py:108
  38.2 4.4 %convolution_add_fusion = f32[240,2152]{1,0:T(8,128)S(1)} fusion(bf16[1152,2152]{0,1:T(8,128)(2,1)} %param.22, f32[2152]{0:T(1024)S(1)} %copy-done.7, f32[240,1152]{1,0:T(8,128)S(1)} %reshape.240, f32[1152]{0:T(1024)S(1)} %copy-done.8, f32[1152]{0:T(1024)S(1)} %copy-done.6, f32[240]{0:T(256)S(1)} %rsqrt.44, f32[240]{0:T(256)S(1)} %div.65), kind=kOutput, calls=%fused_computation.2 | convolution fusion | flops 1191868800 | bytes 8149792 | tf_op jit(solution)/shard_map/dot_general | solution.py:112
  42.6 4.7 %fusion.45 = (f32[2152]{0:T(1024)S(1)}, bf16[240,2152]{1,0:T(8,128)(2,1)S(1)}) fusion(f32[240,2152]{1,0:T(8,128)S(1)} %convolution_add_fusion, bf16[240,1152]{1,0:T(8,128)(2,1)S(1)} %reshape.238, bf16[2152,1152]{1,0:T(8,128)(2,1)} %param.24), kind=kOutput, calls=%fused_computation.101 | convolution fusion | flops 1200297344 | bytes 8618656 | tf_op jit(solution)/shard_map/dot_general | solution.py:114
  47.4 1.6 %fusion.7 = f32[240,1152]{1,0:T(8,128)S(1)} fusion(bf16[1152,2152]{0,1:T(8,128)(2,1)S(1)} %bitcast.108, bf16[240,2152]{1,0:T(8,128)(2,1)S(1)} %get-tuple-element.31), kind=kOutput, calls=%fused_computation.14 | convolution fusion | flops 1189969920 | bytes 7097088 | tf_op jit(solution)/shard_map/dot_general | solution.py:125
  49.1 1.8 %copy.70 = f32[4,60,1152]{2,0,1:T(4,128)} copy(f32[4,60,1152]{2,1,0:T(8,128)S(1)} %reshape.239) | data formatting | bytes 2211840 | tf_op jit(solution)/shard_map/reshape | solution.py:131
  51.4 0.6 fusion.21
  52.6 18.3 %all-reduce.3.cloned.1.call-done = f32[4,60,1152]{2,0,1:T(4,128)} async-done(((f32[4,60,1152]{2,0,1:T(4,128)}), f32[4,60,1152]{2,0,1:T(4,128)}) %all-reduce.3.cloned.1.call-update) | async-done | bytes 1105936 | tf_op jit(solution)/shard_map/psum | solution.py:131
  70.9 2.5 %fusion.32 = (f32[1152]{0:T(1024)S(1)}, f32[2,60]{0,1:T(8,128)S(1)}, f32[1152]{0:T(1024)S(1)}) fusion(f32[2,60]{0,1:T(8,128)S(1)} %copy.74, f32[2,60]{0,1:T(8,128)S(1)} %broadcast_multiply_fusion.1, f32[4,60,1152]{2,0,1:T(4,128)} %all-reduce.3.cloned.1.call-done, s32[]{:T(128)S(6)} %select_n.59, bf16[1,4,60,1152]{3,1,2,0:T(4,128)(2,1)S(1)} %copy-done, ...), kind=kLoop, calls=%fused_computation.53 | loop fusion | flops 1241736 | bytes 844708 | tf_op jit(solution)/shard_map/transpose(jvp())/reduce_sum | solution.py:49
  73.5 41.2 %all-reduce = (f32[6,1152]{1,0:T(8,128)S(1)}, f32[4304]{0:T(1024)S(1)}) all-reduce(f32[6,1152]{1,0:T(8,128)S(1)} %stack.27, f32[4304]{0:T(1024)S(1)} %dynamic_update_slice.3), channel_id=1, replica_groups=mesh['seq'=4,'dp'=4,'enc'=2] {'seq','dp','enc'}, use_global_device_ids=true, to_apply=%region_26.27 | all-reduce | flops 11216 | bytes 89728 | tf_op jit(solution)/shard_map/psum | solution.py:143
  114.7 0.6 broadcast_multiply_fusion
  115.3 0.6 broadcast_multiply_fusion.4
  116.1 2.3 %fusion.41 = (f32[2,60]{0,1:T(8,128)S(1)}, f32[2,60,1152]{2,0,1:T(2,128)S(1)}) fusion(f32[2,60]{0,1:T(8,128)S(1)} %copy.76, f32[2,60]{0,1:T(8,128)S(1)} %broadcast_multiply_fusion.1, bf16[1,4,60,1152]{3,1,2,0:T(4,128)(2,1)S(1)} %copy-done, s32[]{:T(128)S(6)} %select_n.59, f32[2,60]{0,1:T(8,128)S(1)} %copy.74, f32[1152]{0:T(1024)S(1)} %copy-done.6, ...), kind=kLoop, calls=%fused_computation.98 | loop fusion | flops 1105800 | bytes 1388932 | tf_op jit(solution)/shard_map/transpose(jvp())/reduce_sum | solution.py:19
  118.5 1.1 fusion.33
  (78 shorter events, 4.2 us)
Async XLA Ops:
  7.2 5.6 %copy-start.2 = (bf16[1,2,48,1152]{3,2,1,0:T(8,128)(2,1)S(1)}, bf16[1,2,48,1152]{3,2,1,0:T(8,128)(2,1)}, u32[]{:S(2)}) copy-start(bf16[1,2,48,1152]{3,2,1,0:T(8,128)(2,1)} %param.14) | copy-start | bytes 663556
  7.2 63.7 %all-reduce.3.cloned.1.call-start = ((), (), s32[]{:S(2)}) async-start(), calls=%async_computation | async-start | bytes 2211840 | tf_op jit(solution)/shard_map/psum | solution.py:131
  9.9 16.7 %copy-start.1 = (bf16[1,2,60,1152]{3,1,2,0:T(2,128)(2,1)S(1)}, bf16[1,2,60,1152]{3,1,2,0:T(2,128)(2,1)}, u32[]{:S(2)}) copy-start(bf16[1,2,60,1152]{3,1,2,0:T(2,128)(2,1)} %param.19) | copy-start | bytes 829444
  11.5 16.1 %copy-start.3 = (f32[1152]{0:T(1024)S(1)}, f32[1152]{0:T(1024)}, u32[]{:S(2)}) copy-start(f32[1152]{0:T(1024)} %param.25) | copy-start | bytes 13828
  11.5 16.1 %copy-start.4 = (f32[1152]{0:T(1024)S(1)}, f32[1152]{0:T(1024)}, u32[]{:S(2)}) copy-start(f32[1152]{0:T(1024)} %param.26) | copy-start | bytes 13828
  12.7 17.0 %copy-start.5 = (f32[1152]{0:T(1024)S(1)}, f32[1152]{0:T(1024)}, u32[]{:S(2)}) copy-start(f32[1152]{0:T(1024)} %param.27) | copy-start | bytes 13828
  35.1 3.1 %copy-start.6 = (f32[1152]{0:T(1024)S(1)}, f32[1152]{0:T(1024)}, u32[]{:S(2)}) copy-start(f32[1152]{0:T(1024)} %param.20) | copy-start | bytes 13828
  35.1 3.1 %copy-start.7 = (f32[2152]{0:T(1024)S(1)}, f32[2152]{0:T(1024)}, u32[]{:S(2)}) copy-start(f32[2152]{0:T(1024)} %param.23) | copy-start | bytes 25828
  35.1 3.1 %copy-start.8 = (f32[1152]{0:T(1024)S(1)}, f32[1152]{0:T(1024)}, u32[]{:S(2)}) copy-start(f32[1152]{0:T(1024)} %param.21) | copy-start | bytes 13828
  38.2 9.1 %slice-start = ((s8[4958208]{0:T(1024)(128)(4,1)}), s8[4194304]{0:T(1024)(128)(4,1)S(1)}, s32[]{:S(2)}) async-start(s8[4958208]{0:T(1024)(128)(4,1)} %bitcast.107), calls=%async_computation.1 | async-start | bytes 8388608
  42.6 4.7 %slice-start.1 = ((s8[4958208]{0:T(1024)(128)(4,1)}), s8[763904]{0:T(1024)(128)(4,1)S(1)}, s32[]{:S(2)}) async-start(s8[4958208]{0:T(1024)(128)(4,1)} %bitcast.107), calls=%async_computation.2 | async-start | bytes 1527808
  49.1 1.8 %copy-start = (bf16[1,4,60,1152]{3,1,2,0:T(4,128)(2,1)S(1)}, bf16[1,4,60,1152]{3,1,2,0:T(4,128)(2,1)}, u32[]{:S(2)}) copy-start(bf16[1,4,60,1152]{3,1,2,0:T(4,128)(2,1)} %param.18) | copy-start | bytes 1658884
Sparse Core Ops, SparseCore 0:
  51.0 19.8 all-reduce.2
where the time goes:
time: 127 us; the launch traced here: 126 us
  blocking collectives  57.4 us (45%)
  other arithmetic  19 us (15%)
  waiting for transfers between devices  18.3 us (14%)
  between operations  14.4 us (11%)
  matrix products  10.7 us (8%)
  local copies, waits for them, and re-layouts  6.55 us (5%)
    psum x1, blocking collectives, body(): norm_sum, fc1_sum = lax.psum((norm_part, fc1_full), ('seq', 'dp', 'enc'))  41.2 us
    psum x1, waiting for transfers between devices, body(): summed = lax.psum(product.reshape(PATCH_GROUP, CAP_TOK, D), 'enc')  18.3 us
    all_gather x1, blocking collectives, body(): portion = lax.all_gather(own_rows, 'seq', axis=1, tiled=True)  13.7 us
    dot_general x1, matrix products, body(): lax.dot_general(all_res.reshape(-1, D), fc2_weight, (((1,), (1,)), ((), (...  4.7 us
    dot_general x1, matrix products, body(): jnp.dot(normed.reshape(-1, D), fc1_weight, preferred_element_type=jnp.flo...  4.4 us
    reduce_sum x2, other arithmetic, layer_norm(): centred = values - row_mean  3.14 us
    reduce_sum x3, other arithmetic, layer_norm(): jnp.mean(centred * centred, axis=-1, keepdims=True) + EPSILON  2.67 us
    all_gather x1, blocking collectives, body(): all_res = lax.all_gather(res_wire, 'enc', axis=0, tiled=True)  2.54 us
  transfers between devices with their start and end apart: 1, of which 1 were waited for; matrix products, arithmetic and copies ran while one was open for 1% of the time, Pallas kernels for 0%

commit v1 on v0

--- a/solution.py
+++ b/solution.py
@@ -12,6 +12,12 @@
 EPSILON = 1e-06
 SLOPE_K = math.sqrt(2.0 / math.pi)
 CUBIC = 0.044715
+
+
+def summed_here(block, axis):
+    terms = lax.all_gather(block, axis, axis=0, tiled=False)
+    total = terms.sum(axis=0)
+    return total
 
 
 def layer_norm(values):
@@ -128,7 +134,7 @@
         (((1,), (1,)), ((), ())),
         preferred_element_type=jnp.float32,
     )
-    summed = lax.psum(product.reshape(PATCH_GROUP, CAP_TOK, D), "enc")
+    summed = summed_here(product.reshape(PATCH_GROUP, CAP_TOK, D), "enc")
     upstream = lax.dynamic_slice_in_dim(summed, core_index * own_patches, own_patches, 0)
     own_input = lax.dynamic_slice_in_dim(input_rows, core_index * own_patches, own_patches, 0)
     input_grad, pre_scale_grad, pre_shift_grad = pre_back(own_input, pre_gain, pre_bias, upstream)

time: 127 us -> 118 us (0.929)
  waiting for transfers between devices: 18.3 us -> 9.54 us
    psum x1 -> x0, waiting for transfers between devices: 18.3 us -> none  [body(): summed = lax.psum(product.reshape(PATCH_GROUP, CAP_TOK, D), 'enc')]
    all_gather x0 -> x1, waiting for transfers between devices: none -> 9.53 us  [summed_here(): terms = lax.all_gather(block, axis, axis=0, tiled=False)]
    reduce_sum x0 -> x1, other arithmetic: none -> 2.42 us  [summed_here(): total = terms.sum(axis=0)]
    reshape x2 -> x0, local copies, waits for them, and re-layouts: 1.88 us -> none  [body(): summed = lax.psum(product.reshape(PATCH_GROUP, CAP_TOK, D), 'enc')]
    another operation x0 -> x2, local copies, waits for them, and re-layouts: none -> 1.83 us  [summed_here(): terms = lax.all_gather(block, axis, axis=0, tiled=False)]
where the time goes in v1:
time: 118 us
  blocking collectives  57.6 us (49%)
  other arithmetic  18.9 us (16%)
  between operations  14.4 us (12%)
  matrix products  10.7 us (9%)
  waiting for transfers between devices  9.54 us (8%)
  local copies, waits for them, and re-layouts  6.51 us (6%)
    psum x1, blocking collectives, body(): norm_sum, fc1_sum = lax.psum((norm_part, fc1_full), ('seq', 'dp', 'enc'))  41.4 us
    all_gather x1, blocking collectives, body(): portion = lax.all_gather(own_rows, 'seq', axis=1, tiled=True)  13.7 us
    all_gather x1, waiting for transfers between devices, summed_here(): terms = lax.all_gather(block, axis, axis=0, tiled=False)  9.53 us
    dot_general x1, matrix products, body(): lax.dot_general(all_res.reshape(-1, D), fc2_weight, (((1,), (1,)), ((), (...  4.71 us
    dot_general x1, matrix products, body(): jnp.dot(normed.reshape(-1, D), fc1_weight, preferred_element_type=jnp.flo...  4.4 us
    reduce_sum x3, other arithmetic, layer_norm(): jnp.mean(centred * centred, axis=-1, keepdims=True) + EPSILON  2.67 us
    all_gather x1, blocking collectives, body(): all_res = lax.all_gather(res_wire, 'enc', axis=0, tiled=True)  2.54 us
    reduce_sum x1, other arithmetic, summed_here(): total = terms.sum(axis=0)  2.42 us
  transfers between devices with their start and end apart: 1, of which 1 were waited for; matrix products, arithmetic and copies ran while one was open for 1% of the time, Pallas kernels for 0%

profile of v1, /device:TPU:0, one launch (start us, length us, event | category | flops | bytes accessed | tf_op | source)
XLA Modules:
  0.0 117.7 jit_solution(6779867924873145190)
XLA Ops:
  7.2 0.9 select_reduce_fusion.2
  8.5 1.3 %convert_reduce_fusion.2 = f32[4,60]{0,1:T(8,128)S(1)} fusion(bf16[1,4,60,1152]{3,1,2,0:T(4,128)(2,1)} %param.18), kind=kLoop, calls=%fused_computation.44 | loop fusion | flops 552720 | bytes 553920 | tf_op jit(solution)/shard_map/reduce_sum | solution.py:24
  9.9 1.6 %fusion.6 = f32[4,60]{0,1:T(8,128)S(1)} fusion(bf16[1,4,60,1152]{3,1,2,0:T(4,128)(2,1)} %param.18, f32[4,60]{0,1:T(8,128)S(1)} %broadcast_multiply_fusion.2), kind=kLoop, calls=%fused_computation.12 | loop fusion | flops 1105680 | bytes 554880 | tf_op jit(solution)/shard_map/reduce_sum | solution.py:26
  11.6 1.1 copy.70
  12.9 13.7 %all-gather = bf16[1,2,192,1152]{3,1,0,2:T(2,128)(2,1)S(1)} all-gather(bf16[1,2,48,1152]{3,1,0,2:T(2,128)(2,1)S(1)} %copy.56), channel_id=2, replica_groups=mesh['seq'=4,'dp'=4,'enc'=2] {'seq'}, dimensions={2}, use_global_device_ids=true | all-gather | bytes 1105920 | tf_op jit(solution)/shard_map/all_gather | solution.py:105
  27.6 0.7 multiply_reduce_fusion.1
  28.6 1.2 gather_fusion
  29.7 1.7 %fusion.27 = (f32[1152]{0:T(1024)S(1)}, f32[2,60]{0,1:T(8,128)S(1)}, bf16[60,2,1152]{2,1,0:T(2,128)(2,1)S(1)}) fusion(f32[2,60]{0,1:T(8,128)S(1)} %copy.62, f32[1152]{0:T(1024)S(1)} %copy-done.4, f32[1152]{0:T(1024)S(1)} %copy-done.3, f32[2,60]{0,1:T(8,128)S(1)} %copy.60, f32[2,60]{0,1:T(8,128)S(1)} %broadcast_multiply_fusion.3, ...), kind=kLoop, calls=%fused_computation.43 | loop fusion | flops 1934088 | bytes 849912 | tf_op jit(solution)/shard_map/transpose(jvp())/reduce_sum | solution.py:44
  31.7 1.9 %multiply_reduce_fusion = (f32[1152]{0:T(1024)S(1)}, f32[2,60]{0,1:T(8,128)S(1)}, f32[1152]{0:T(1024)S(1)}, f32[2,60,1152]{2,0,1:T(2,128)S(1)}) fusion(bf16[1,2,60,1152]{3,1,2,0:T(2,128)(2,1)S(1)} %copy-done.1, f32[2,60]{0,1:T(8,128)S(1)} %copy.60, f32[2,60]{0,1:T(8,128)S(1)} %broadcast_multiply_fusion.3, f32[1152]{0:T(1024)S(1)} %copy-done.3, ...), kind=kLoop, calls=%fused_computation.45 | loop fusion | flops 2347656 | bytes 1131360 | tf_op jit(solution)/shard_map/transpose(jvp())/reduce_sum | solution.py:44
  33.8 0.8 fusion.42
  35.1 2.5 %all_gather.10 = bf16[4,60,1152]{2,1,0:T(8,128)(2,1)S(1)} all-gather(bf16[2,60,1152]{2,1,0:T(8,128)(2,1)S(1)} %copy.69), channel_id=1, replica_groups=mesh['seq'=4,'dp'=4,'enc'=2] {'enc'}, dimensions={0}, use_global_device_ids=true | all-gather | bytes 829440 | tf_op jit(solution)/shard_map/all_gather | solution.py:114
  38.2 4.4 %convolution_add_fusion = f32[240,2152]{1,0:T(8,128)S(1)} fusion(bf16[1152,2152]{0,1:T(8,128)(2,1)} %param.22, f32[2152]{0:T(1024)S(1)} %copy-done.7, f32[240,1152]{1,0:T(8,128)S(1)} %reshape.236, f32[1152]{0:T(1024)S(1)} %copy-done.8, f32[1152]{0:T(1024)S(1)} %copy-done.6, f32[240]{0:T(256)S(1)} %rsqrt.44, f32[240]{0:T(256)S(1)} %div.65), kind=kOutput, calls=%fused_computation.2 | convolution fusion | flops 1191868800 | bytes 8149792 | tf_op jit(solution)/shard_map/dot_general | solution.py:118
  42.6 4.7 %fusion.45 = (f32[2152]{0:T(1024)S(1)}, bf16[240,2152]{1,0:T(8,128)(2,1)S(1)}) fusion(f32[240,2152]{1,0:T(8,128)S(1)} %convolution_add_fusion, bf16[240,1152]{1,0:T(8,128)(2,1)S(1)} %reshape.235, bf16[2152,1152]{1,0:T(8,128)(2,1)} %param.24), kind=kOutput, calls=%fused_computation.101 | convolution fusion | flops 1200297344 | bytes 8618656 | tf_op jit(solution)/shard_map/dot_general | solution.py:120
  47.4 1.6 %fusion.7 = f32[240,1152]{1,0:T(8,128)S(1)} fusion(bf16[1152,2152]{0,1:T(8,128)(2,1)S(1)} %bitcast.108, bf16[240,2152]{1,0:T(8,128)(2,1)S(1)} %get-tuple-element.31), kind=kOutput, calls=%fused_computation.14 | convolution fusion | flops 1189969920 | bytes 7097088 | tf_op jit(solution)/shard_map/dot_general | solution.py:131
  49.1 1.7 %copy.74 = f32[1,4,60,1152]{3,1,2,0:T(4,128)} copy(f32[1,4,60,1152]{3,2,1,0:T(8,128)S(1)} %all_gather_reshape.3) | data formatting | bytes 2211840 | tf_op jit(solution)/shard_map/all_gather;reshape | solution.py:18
  51.3 0.6 fusion.21
  52.5 9.5 %all-gather.3.cloned.1.call-done = f32[2,4,60,1152]{3,1,2,0:T(4,128)} async-done(((f32[1,4,60,1152]{3,1,2,0:T(4,128)}), f32[2,4,60,1152]{3,1,2,0:T(4,128)}) %all-gather.3.cloned.1.call-update) | async-done | bytes 2211856 | tf_op jit(solution)/shard_map/all_gather | solution.py:18
  62.0 2.4 %reduce_sum.284 = f32[4,60,1152]{2,0,1:T(4,128)S(1)} reduce(f32[2,4,60,1152]{3,1,2,0:T(4,128)} %all-gather.3.cloned.1.call-done, f32[]{:T(128)} %constant.33.clone.1), dimensions={0}, to_apply=%region_15.16 | reduce | flops 276480 | bytes 3317764 | tf_op jit(solution)/shard_map/reduce_sum | solution.py:19
  64.5 1.3 %fusion.32 = (f32[1152]{0:T(1024)S(1)}, f32[2,60]{0,1:T(8,128)S(1)}, f32[1152]{0:T(1024)S(1)}) fusion(f32[2,60]{0,1:T(8,128)S(1)} %copy.80, f32[2,60]{0,1:T(8,128)S(1)} %broadcast_multiply_fusion.1, f32[4,60,1152]{2,0,1:T(4,128)S(1)} %reduce_sum.284, s32[]{:T(128)S(6)} %select_n.59, bf16[1,4,60,1152]{3,1,2,0:T(4,128)(2,1)S(1)} %copy-done, f32[1152]{0:T(1024)S(1)} %copy-done.6), kind=kLoop, calls=%fused_computation.53 | loop fusion | flops 1241736 | bytes 844708 | tf_op jit(solution)/shard_map/transpose(jvp())/reduce_sum | solution.py:55
  65.8 41.4 %all-reduce = (f32[6,1152]{1,0:T(8,128)S(1)}, f32[4304]{0:T(1024)S(1)}) all-reduce(f32[6,1152]{1,0:T(8,128)S(1)} %stack.27, f32[4304]{0:T(1024)S(1)} %dynamic_update_slice.3), channel_id=1, replica_groups=mesh['seq'=4,'dp'=4,'enc'=2] {'seq','dp','enc'}, use_global_device_ids=true, to_apply=%region_26.27 | all-reduce | flops 11216 | bytes 89728 | tf_op jit(solution)/shard_map/psum | solution.py:149
  107.2 0.6 broadcast_multiply_fusion
  107.9 0.6 broadcast_multiply_fusion.4
  108.7 1.1 fusion.41
  109.8 1.1 fusion.33
  (79 shorter events, 4.7 us)
Async XLA Ops:
  7.2 5.6 %copy-start.2 = (bf16[1,2,48,1152]{3,2,1,0:T(8,128)(2,1)S(1)}, bf16[1,2,48,1152]{3,2,1,0:T(8,128)(2,1)}, u32[]{:S(2)}) copy-start(bf16[1,2,48,1152]{3,2,1,0:T(8,128)(2,1)} %param.14) | copy-start | bytes 663556
  7.2 54.9 %all-gather.3.cloned.1.call-start = ((), (), s32[]{:S(2)}) async-start(), calls=%async_computation | async-start | bytes 3317760 | tf_op jit(solution)/shard_map/all_gather | solution.py:18
  9.9 16.7 %copy-start.1 = (bf16[1,2,60,1152]{3,1,2,0:T(2,128)(2,1)S(1)}, bf16[1,2,60,1152]{3,1,2,0:T(2,128)(2,1)}, u32[]{:S(2)}) copy-start(bf16[1,2,60,1152]{3,1,2,0:T(2,128)(2,1)} %param.19) | copy-start | bytes 829444
  11.5 16.1 %copy-start.3 = (f32[1152]{0:T(1024)S(1)}, f32[1152]{0:T(1024)}, u32[]{:S(2)}) copy-start(f32[1152]{0:T(1024)} %param.25) | copy-start | bytes 13828
  11.5 16.1 %copy-start.4 = (f32[1152]{0:T(1024)S(1)}, f32[1152]{0:T(1024)}, u32[]{:S(2)}) copy-start(f32[1152]{0:T(1024)} %param.26) | copy-start | bytes 13828
  12.7 17.0 %copy-start.5 = (f32[1152]{0:T(1024)S(1)}, f32[1152]{0:T(1024)}, u32[]{:S(2)}) copy-start(f32[1152]{0:T(1024)} %param.27) | copy-start | bytes 13828
  35.1 3.1 %copy-start.6 = (f32[1152]{0:T(1024)S(1)}, f32[1152]{0:T(1024)}, u32[]{:S(2)}) copy-start(f32[1152]{0:T(1024)} %param.20) | copy-start | bytes 13828
  35.1 3.1 %copy-start.7 = (f32[2152]{0:T(1024)S(1)}, f32[2152]{0:T(1024)}, u32[]{:S(2)}) copy-start(f32[2152]{0:T(1024)} %param.23) | copy-start | bytes 25828
  35.1 3.1 %copy-start.8 = (f32[1152]{0:T(1024)S(1)}, f32[1152]{0:T(1024)}, u32[]{:S(2)}) copy-start(f32[1152]{0:T(1024)} %param.21) | copy-start | bytes 13828
  38.2 9.2 %slice-start = ((s8[4958208]{0:T(1024)(128)(4,1)}), s8[4194304]{0:T(1024)(128)(4,1)S(1)}, s32[]{:S(2)}) async-start(s8[4958208]{0:T(1024)(128)(4,1)} %bitcast.107), calls=%async_computation.1 | async-start | bytes 8388608
  42.6 4.7 %slice-start.1 = ((s8[4958208]{0:T(1024)(128)(4,1)}), s8[763904]{0:T(1024)(128)(4,1)S(1)}, s32[]{:S(2)}) async-start(s8[4958208]{0:T(1024)(128)(4,1)} %bitcast.107), calls=%async_computation.2 | async-start | bytes 1527808
  49.1 1.8 %copy-start = (bf16[1,4,60,1152]{3,1,2,0:T(4,128)(2,1)S(1)}, bf16[1,4,60,1152]{3,1,2,0:T(4,128)(2,1)}, u32[]{:S(2)}) copy-start(bf16[1,4,60,1152]{3,1,2,0:T(4,128)(2,1)} %param.18) | copy-start | bytes 1658884
Sparse Core Ops, SparseCore 0:
  51.0 11.0 all-gather.2
